TPU v7x, 512 devices: a whole 4x8x8 slice. The times are simulated.
512 devices in a mesh: dp: 64 (over y_lo, z, core), tensor: 8 (over y_hi, x).
Axes of the slice: x: 4, y: 8 (y_hi: 2, y_lo: 4; y = y_hi * 4 + y_lo), z: 8, core: 2. Of those that a mesh axis runs over, the one named last changes fastest.
Arguments:
- hidden_rows: bfloat16 [4096, 16384], P('dp', 'tensor')
- norm_gain: float32 [16384], P('tensor'), may hold values from 0.5 to 1.5
- key_weight: bfloat16 [512, 16384], P('dp', 'tensor'), may hold values from -0.046875 to 0.046875
- cotangent: bfloat16 [64, 128, 512], P('dp'), may hold values from -16 to 16
- accepted_counts: int32 [64], P('dp'), may hold values from 16 to 64, as said below
- destination: int32 [4096], P('dp'), may hold values from 0 to 63, as said below
Outputs:
- keys: bfloat16 [64, 128, 512], P('dp')
- key_weight_grad: float32 [512, 16384], P('dp', 'tensor')
- gain_grad: float32 [16384], P('tensor')
Inputs may be any that keep to these rules, and one draw needn't show every extreme that they name: `accepted_counts`: rows 0 to the count minus 1 of a replica are accepted; in every draw one replica accepts all its rows and another a quarter of them. `destination`: among one replica's 64 rows no shard is named more than 2 times; in every draw one shard is named exactly 2 times by every replica, all within the first quarter of that replica's rows.
All inputs are finite; a program needn't handle non-finite values.
Results may differ from a plain program's by a relative error of at most 0.0051.
Values may be sent and summed in bfloat16 or wider, within the bound.
A program may use at most 64 MiB of HBM per device.

v0:
```python
import math

import jax
import jax.numpy as jnp
from jax import lax
from jax.sharding import PartitionSpec as P

D = 16384


EPSILON = 1e-05


def slot_layout(dest_rows, count, groups, capacity):
    row_total = dest_rows.shape[0]
    row_order = lax.broadcasted_iota(jnp.int32, (row_total,), 0)
    onehot = (dest_rows[:, None] == lax.broadcasted_iota(jnp.int32, (row_total, groups), 1)).astype(
        jnp.int32
    )
    before = jnp.cumsum(onehot, axis=0) - onehot
    slot_rank = jnp.sum(before * onehot, axis=1)
    accepted = row_order < count
    position = dest_rows * capacity + slot_rank
    filler = jnp.full((groups * capacity,), row_total, jnp.int32)
    filler = filler.at[jnp.where(accepted, position, groups * capacity)].set(row_order, mode="drop")
    return (accepted, position, filler)


def with_blank(source_table):
    return jnp.concatenate(
        [source_table, jnp.zeros((1, source_table.shape[1]), source_table.dtype)], axis=0
    )


def on_device(hidden_rows, norm_gain, key_weight, cotangent, accepted_counts, destination):
    replicas = lax.axis_size("dp")
    own_rows = hidden_rows.shape[0]
    capacity = 2 * own_rows // replicas
    accepted, position, filler = slot_layout(destination, accepted_counts[0], replicas, capacity)
    row_data = lax.all_to_all(
        with_blank(hidden_rows)[filler], "dp", split_axis=0, concat_axis=0, tiled=True
    )
    row_cot = cotangent[0]
    row_float = row_data.astype(jnp.float32)
    squares = lax.psum(jnp.sum(row_float * row_float, axis=1), "tensor")
    normed = (row_float * lax.rsqrt(squares / D + EPSILON)[:, None] * norm_gain[None, :]).astype(
        jnp.bfloat16
    )
    weights_whole = lax.all_gather(key_weight, "dp", axis=0, tiled=True)
    partial_value = lax.dot_general(
        normed, weights_whole, (((1,), (1,)), ((), ())), preferred_element_type=jnp.float32
    )
    backward = jnp.dot(row_cot, weights_whole, preferred_element_type=jnp.float32)
    row_keys = lax.psum(partial_value, "tensor").astype(jnp.bfloat16)
    factor = 1.0 / math.sqrt(own_rows * replicas)
    grad_weight = (
        lax.psum_scatter(
            lax.dot_general(
                row_cot, normed, (((0,), (0,)), ((), ())), preferred_element_type=jnp.float32
            ),
            "dp",
            scatter_dimension=0,
            tiled=True,
        )
        * factor
    )
    gain_term = jnp.sum(backward * normed.astype(jnp.float32), axis=0)
    grad_gain = lax.psum(gain_term, "dp") * factor / norm_gain
    return (row_keys[None], grad_weight, grad_gain)


def solution(mesh):
    return jax.shard_map(
        on_device,
        mesh=mesh,
        in_specs=(
            P("dp", "tensor"),
            P("tensor"),
            P("dp", "tensor"),
            P("dp", None, None),
            P("dp"),
            P("dp"),
        ),
        out_specs=(P("dp", None, None), P("dp", "tensor"), P("tensor")),
        check_vma=False,
    )
```

profile of v0, /device:TPU:1, one launch (start us, length us, event | category | flops | bytes accessed | tf_op | source)
XLA Modules:
  0.0 432.0 jit_solution(2184907873028048254)
XLA Ops:
  7.2 0.0 copy-start
  7.2 0.0 all-gather.2.cloned.1.call-start
  7.2 0.7 all-gather.2.cloned.1.call-update
  7.9 0.0 reduce-scatter.4.cloned.1.call-start
  8.6 0.7 fusion.3
  9.3 0.1 reduce_window_sum.11
  9.4 1.0 concatenate.3
  10.4 0.8 select_reduce_fusion
  11.3 0.7 compare_select_fusion.1
  11.9 0.8 scatter_custom_fusion
  12.7 0.9 gather_fusion
  13.7 0.0 copy-start.2
  13.7 0.3 all_to_all.6
  14.0 33.1 %all_to_all.9 = bf16[64,2,2048]{2,1,0:T(2,128)(2,1)S(1)} all-to-all(bf16[64,2,2048]{2,1,0:T(2,128)(2,1)S(1)} %all_to_all.6), channel_id=1, replica_groups=mesh['dp'=64,'tensor'=8] {'dp'}, dimensions={0} | all-to-all | bytes 1048576 | tf_op jit(solution)/shard_map/all_to_all | solution.py:40
  47.2 0.6 multiply_reduce_fusion
  47.8 0.1 reduce_sum.31
  47.9 25.0 %psum.21 = f32[128]{0:T(128)S(1)} all-reduce(f32[128]{0:T(128)S(1)} %reduce_sum.31), channel_id=1, replica_groups=mesh['dp'=64,'tensor'=8] {'tensor'}, use_global_device_ids=true, to_apply=%region_4.5 | all-reduce | flops 128 | bytes 1024 | tf_op jit(solution)/shard_map/psum | solution.py:45
  73.0 0.1 mul.64
  73.1 0.0 copy-done.2
  73.1 0.6 multiply_convert_fusion
  73.7 0.2 convert_element_type.34
  73.9 0.0 copy-done
  73.9 2.7 convolution_bitcast_fusion
  76.6 5.4 %copy.12 = f32[512,2048]{1,0:T(8,128)} copy(f32[512,2048]{0,1:T(8,128)} %convolution_bitcast_fusion) | data formatting | bytes 8388608
  82.0 0.0 reduce-scatter.4.cloned.1.call-update
  82.0 0.1 reshape.23
  82.2 57.2 %all-gather.2.cloned.1.call-done = bf16[512,2048]{1,0:T(8,128)(2,1)} async-done(((bf16[8,2048]{1,0:T(8,128)(2,1)}), bf16[512,2048]{1,0:T(8,128)(2,1)}) %all-gather.2.cloned.1.call-update) | async-done | bytes 2097168 | tf_op jit(solution)/shard_map/all_gather | solution.py:49
  139.4 0.0 copy-start.1
  139.4 2.6 fusion.6
  141.9 0.0 copy-done.1
  142.0 0.6 fusion
  142.5 135.3 %psum.23 = f32[2048]{0:T(1024)S(1)} all-reduce(f32[2048]{0:T(1024)S(1)} %fusion), channel_id=1, replica_groups=mesh['dp'=64,'tensor'=8] {'dp'}, use_global_device_ids=true, to_apply=%region_8.9 | all-reduce | flops 2048 | bytes 16384 | tf_op jit(solution)/shard_map/psum | solution.py:68
  277.9 0.6 multiply_divide_fusion
  278.5 48.9 %all-reduce.2 = bf16[128,512]{1,0:T(8,128)(2,1)} all-reduce(f32[128,512]{1,0:T(8,128)S(1)} %fusion.6), channel_id=1, replica_groups=mesh['dp'=64,'tensor'=8] {'tensor'}, use_global_device_ids=true, to_apply=%region_5.6 | all-reduce | flops 65536 | bytes 393216 | tf_op jit(solution)/shard_map/psum | solution.py:54
  327.4 95.6 %reduce-scatter.4.cloned.1.call-done = f32[8,2048]{1,0:T(8,128)} async-done(((f32[512,2048]{1,0:T(8,128)}), f32[8,2048]{1,0:T(8,128)}) %reduce-scatter.4.cloned.1.call-update) | async-done | bytes 65552
  423.0 1.2 copy.13
  424.1 0.1 broadcast_multiply_fusion
  424.2 0.9 copy.11
  (4 shorter events, 0.0 us)
Async XLA Ops:
  7.2 66.8 %copy-start = (bf16[1,128,512]{2,1,0:T(8,128)(2,1)S(1)}, bf16[1,128,512]{2,1,0:T(8,128)(2,1)}, u32[]{:S(2)}) copy-start(bf16[1,128,512]{2,1,0:T(8,128)(2,1)} %param.9) | copy-start | bytes 393220
  7.2 132.2 %all-gather.2.cloned.1.call-start = ((), (), s32[]{:S(2)}) async-start(), calls=%async_computation.2 | async-start | bytes 2129920 | tf_op jit(solution)/shard_map/all_gather | solution.py:49
  7.9 415.1 %reduce-scatter.4.cloned.1.call-start = ((), (), s32[]{:S(2)}) async-start(), calls=%async_computation.3 | async-start | bytes 4259840
  13.7 59.4 %copy-start.2 = (f32[2048]{0:T(1024)S(1)}, f32[2048]{0:T(1024)}, u32[]{:S(2)}) copy-start(f32[2048]{0:T(1024)} %param.7) | copy-start | bytes 24580
  139.4 2.6 copy-start.1
Sparse Core Ops, SparseCore 0:
  10.2 129.1 all-gather.1
  142.2 280.7 reduce-scatter.3
where the time goes:
time: 437 us; the launch traced here: 432 us
  blocking collectives  242 us (55%)
  waiting for transfers between devices  153 us (35%)
  between operations  14.8 us (3%)
  local copies, waits for them, and re-layouts  11.1 us (3%)
  matrix products  5.84 us (1%)
    psum x1, blocking collectives, on_device(): grad_gain = lax.psum(gain_term, 'dp') * factor / norm_gain  135 us
    unnamed x3, waiting for transfers between devices  96.3 us
    all_gather x1, waiting for transfers between devices, on_device(): weights_whole = lax.all_gather(key_weight, 'dp', axis=0, tiled=True)  57.2 us
    psum x1, blocking collectives, on_device(): row_keys = lax.psum(partial_value, 'tensor').astype(jnp.bfloat16)  48.9 us
    all_to_all x1, blocking collectives, on_device(): lax.all_to_all(with_blank(hidden_rows)[filler], 'dp', split_axis=0, conca...  33.1 us
    psum x1, blocking collectives, on_device(): squares = lax.psum(jnp.sum(row_float * row_float, axis=1), 'tensor')  25 us
  transfers between devices with their start and end apart: 2, of which 2 were waited for; matrix products, arithmetic and copies ran while one was open for 4% of the time, Pallas kernels for 0%

commit v1 on v0

v1 whole, which is shorter than its diff:
```python
import functools
import math

import jax
import jax.numpy as jnp
from jax import lax
from jax.experimental import pallas as pl
from jax.experimental.pallas import tpu as pltpu
from jax.sharding import PartitionSpec as P

EPSILON = 1e-05
F32 = jnp.float32
BF16 = jnp.bfloat16
MESH = pl.DeviceIdType.MESH


def iota(shape, dim):
    return lax.broadcasted_iota(jnp.int32, shape, dim)


def onehot(cond):
    return jnp.where(cond, 1.0, 0.0).astype(BF16)


def kernel(
    dims,
    factor,
    hid,
    gain_ref,
    wsh,
    cot,
    count_ref,
    dest_ref,
    keys_out,
    gw_out,
    gg_out,
    hbuf,
    wown,
    wpart,
    wall,
    cotv,
    cot_a,
    cot_b1,
    cot_s,
    cot_b2,
    cot_r,
    sqb,
    sqc,
    norm,
    gf,
    gs,
    ra,
    rb,
    sa,
    sb,
    gy_s,
    gy_r,
    gc_s,
    gout,
    gz,
    gyb,
    gcb,
    k_part,
    kc_s,
    kc_r,
    kx_s,
    kx_r,
    kh_s,
    kh_r,
    kz_s,
    kz_r,
    ky_s,
    ky_r,
    kout,
    ssem,
    rsem,
    lsem,
):
    NY, NZ, NH, NX = dims
    NT = NH * NX
    dp = lax.axis_index("dp")
    t = lax.axis_index("tensor")
    c = lax.rem(dp, 2)
    z = lax.rem(lax.div(dp, 2), NZ)
    y = lax.div(dp, 2 * NZ)
    x = lax.rem(t, NX)
    h = lax.div(t, NX)
    rows = dest_ref.shape[1]
    slots = 2 * rows
    half = hbuf.shape[2]
    width = half * 2 * NT
    kvw = cotv.shape[1]
    qcols = kvw // NX
    sign = 1 - 2 * c
    LA, LB = NZ // 2, NZ // 2 - 1

    def at_dp(yy, zz, cc):
        return {"dp": (yy * NZ + zz) * 2 + cc}

    partner = at_dp(y, z, 1 - c)
    z_fwd = at_dp(y, lax.rem(z + sign + NZ, NZ), c)
    z_bwd = at_dp(y, lax.rem(z - sign + NZ, NZ), c)

    def zmod(v):
        return lax.rem(v + 2 * NZ, NZ)

    counter = [0]
    sends = []

    def remote(src, dst, dev):
        i = counter[0]
        counter[0] += 1
        d = pltpu.make_async_remote_copy(
            src_ref=src,
            dst_ref=dst,
            send_sem=ssem.at[i],
            recv_sem=rsem.at[i],
            device_id=dev,
            device_id_type=MESH,
        )
        d.start()
        sends.append(d)
        return d

    lcount = [0]

    def local(src, dst):
        i = lcount[0]
        lcount[0] += 1
        d = pltpu.make_async_copy(src, dst, lsem.at[i])
        d.start()
        return d

    own_cols = pl.ds(pl.multiple_of(c * half, half), half)
    other_cols = pl.ds(pl.multiple_of((1 - c) * half, half), half)

    barrier = pltpu.get_barrier_semaphore()
    peers = []
    for d in range(1, NZ):
        peers.append(at_dp(y, lax.rem(z + d, NZ), c))
    for dy in range(NY):
        for dc in range(2):
            if dy or dc:
                peers.append(at_dp(lax.rem(y + dy, NY), z, lax.rem(c + dc, 2)))
    for d in range(1, NT):
        peers.append({"tensor": lax.rem(t + d, NT)})
    for p in peers:
        pl.semaphore_signal(barrier, inc=1, device_id=p, device_id_type=MESH)

    l_cot = local(cot.at[0], cotv)
    l_w = local(wsh.at[:, own_cols], wown)
    l_h = local(hid.at[:, own_cols], hbuf.at[c])

    def perm_zy():
        b = iota((slots, slots), 1)
        bz = (b // 4) % NZ
        by = b // (4 * NZ)
        return onehot(iota((slots, slots), 0) == bz * (4 * NY) + by * 4 + b % 4)

    def perm_yz():
        b = iota((slots, slots), 1)
        bz = b // (4 * NY)
        byc = (b // 2) % (2 * NY)
        return onehot(iota((slots, slots), 0) == byc * (2 * NZ) + bz * 2 + b % 2)

    def perm_out():
        b = iota((slots, slots), 1)
        by = b // (4 * NZ)
        bc = (b // (2 * NZ)) % 2
        bz = (b // 2) % NZ
        return onehot(iota((slots, slots), 0) == by * (4 * NZ) + bz * 4 + bc * 2 + b % 2)

    def dot(a, b):
        return jnp.dot(a, b, preferred_element_type=F32)

    l_cot.wait()
    mixed = dot(perm_zy(), cotv[...]).astype(BF16)
    cot_a[...] = mixed.reshape(NZ, 4 * NY, kvw)

    pl.semaphore_wait(barrier, len(peers))

    r_w = remote(wsh.at[:, other_cols], wpart, partner)
    r_h = remote(hid.at[:, other_cols], hbuf.at[c], partner)

    def z_exchange(src, dst):
        return [
            remote(src.at[lax.rem(z + d, NZ)], dst.at[z], at_dp(y, lax.rem(z + d, NZ), c))
            for d in range(1, NZ)
        ]

    def yc_exchange(src, dst):
        out = []
        for dy in range(NY):
            for dc in range(2):
                if dy or dc:
                    yy, cc = lax.rem(y + dy, NY), lax.rem(c + dc, 2)
                    out.append(remote(src.at[yy * 2 + cc], dst.at[y * 2 + c], at_dp(yy, z, cc)))
        return out

    def recv(copies):
        for d in copies:
            d.wait_recv()

    r_cz = z_exchange(cot_a, cot_b1)
    cot_b1[pl.ds(z, 1)] = cot_a[pl.ds(z, 1)]

    l_w.wait()
    r_w.wait_recv()
    mine, theirs = wown[...].astype(F32), wpart[...].astype(F32)
    low = jnp.where(c == 0, mine, theirs)
    high = jnp.where(c == 0, theirs, mine)
    wall[pl.ds(y, 1), pl.ds(z, 1)] = (
        jnp.concatenate([low, high], axis=0).astype(BF16).reshape(1, 1, 2 * low.shape[0], half)
    )
    r_wy = [
        remote(wall.at[y, z], wall.at[y, z], at_dp(lax.rem(y + d, NY), z, c)) for d in range(1, NY)
    ]

    def w_send(step, d, fwd):
        yy = lax.rem(y - d + NY, NY)
        zz = zmod(z - (step - 1) * sign) if fwd else zmod(z + (step - 1) * sign)
        return remote(wall.at[yy, zz], wall.at[yy, zz], z_fwd if fwd else z_bwd)

    wa, wb = {}, {}

    def w_step(step, d):
        if step <= LA:
            wa[step, d] = w_send(step, d, True)
        if step <= LB:
            wb[step, d] = w_send(step, d, False)

    def w_recv(step, d):
        if step <= LA:
            wa[step, d].wait_recv()
        if step <= LB:
            wb[step, d].wait_recv()

    w_step(1, 0)

    l_h.wait()
    r_h.wait_recv()
    values = hbuf[...].astype(F32).reshape(2 * rows, half)
    sums = jnp.sum(values * values, axis=1, keepdims=True)
    eye2 = iota((2 * rows, 2 * rows), 0) == iota((2 * rows, 2 * rows), 1)
    sqb[pl.ds(t, 1)] = jnp.sum(jnp.where(eye2, sums, 0.0), axis=0, keepdims=True)[None]
    r_sq = [
        remote(sqb.at[t], sqb.at[t], {"tensor": lax.rem(t + d, NT)}) for d in range(1, NT)
    ]

    for d in range(1, NY):
        r_wy[d - 1].wait_recv()
        w_step(1, d)

    recv(r_cz)
    cot_s[...] = (
        dot(perm_yz(), cot_b1[...].reshape(slots, kvw)).astype(BF16).reshape(2 * NY, 2 * NZ, kvw)
    )
    r_cy = yc_exchange(cot_s, cot_b2)
    cot_b2[pl.ds(y * 2 + c, 1)] = cot_s[pl.ds(y * 2 + c, 1)]

    for d in range(NY):
        w_recv(1, d)
        w_step(2, d)

    drow = dest_ref[...]
    sq_shape = (rows, rows)
    eye = iota(sq_shape, 0) == iota(sq_shape, 1)
    dcol = jnp.sum(jnp.where(eye, drow.astype(F32), 0.0), axis=1, keepdims=True).astype(jnp.int32)
    same = dcol == drow
    rank_col = jnp.sum(
        jnp.where(same & (iota(sq_shape, 1) < iota(sq_shape, 0)), 1.0, 0.0), axis=1, keepdims=True
    ).astype(jnp.int32)
    rank_row = jnp.sum(
        jnp.where(same & (iota(sq_shape, 0) < iota(sq_shape, 1)), 1.0, 0.0), axis=0, keepdims=True
    ).astype(jnp.int32)
    count = count_ref[0]

    recv(r_sq)
    total = sqb[0]
    for i in range(1, NT):
        total = total + sqb[i]
    sqc[pl.ds(c, 1)] = total[None]
    r_sc = remote(sqc.at[c], sqc.at[c], partner)

    recv(r_cy)
    d_yc = (dcol // (2 * NZ)) * 2 + dcol % 2
    d_z = (dcol // 2) % NZ
    pos_col = d_yc * (2 * NZ) + d_z * 2 + rank_col
    pick = onehot(
        (iota((rows, slots), 1) == pos_col) & (iota((rows, slots), 0) < count)
    )
    cot_r[pl.ds(c, 1)] = dot(pick, cot_b2[...].reshape(slots, kvw)).astype(BF16)[None]
    r_cr = remote(cot_r.at[c], cot_r.at[c], partner)

    for d in range(NY):
        w_recv(2, d)
        w_step(3, d)

    r_sc.wait_recv()
    total = sqc[0] + sqc[1]
    scale = lax.rsqrt(total / width + EPSILON)
    scale_col = jnp.sum(jnp.where(eye2, scale, 0.0), axis=1, keepdims=True)
    gain_half = gain_ref[:, own_cols]
    norm[...] = (
        hbuf[...].astype(F32).reshape(2 * rows, half) * scale_col * gain_half
    ).astype(BF16)

    r_cr.wait_recv()
    cot2 = cot_r[...].reshape(2 * rows, kvw)
    kb = kvw // NY
    for yy in range(NY):
        part = lax.dot_general(
            cot2[:, yy * kb : (yy + 1) * kb],
            norm[...],
            (((0,), (0,)), ((), ())),
            preferred_element_type=F32,
        ).reshape(NZ, kb // NZ, half)
        gf[yy] = part
        gs[yy] = part.astype(BF16)

    for step in range(3, LA):
        for d in range(NY):
            w_recv(step, d)
            w_step(step + 1, d)

    ga, gb = {}, {}
    za1, zb1 = zmod(z + LA * sign), zmod(z - LB * sign)
    for yy in range(NY):
        ga[1, yy] = remote(gs.at[yy, za1], ra.at[0, yy], z_fwd)
        if LB:
            gb[1, yy] = remote(gs.at[yy, zb1], rb.at[0, yy], z_bwd)

    def g_step(step):
        for yy in range(NY):
            if step <= LA:
                ga[step - 1, yy].wait_recv()
                zz = zmod(z + (LA + 1 - step) * sign)
                own = gf[yy, pl.ds(zz, 1)][0]
                sa[step - 2, yy] = (ra[step - 2, yy].astype(F32) + own).astype(BF16)
                ga[step, yy] = remote(sa.at[step - 2, yy], ra.at[step - 1, yy], z_fwd)
            if step <= LB:
                gb[step - 1, yy].wait_recv()
                zz = zmod(z - (LB + 1 - step) * sign)
                own = gf[yy, pl.ds(zz, 1)][0]
                sb[step - 2, yy] = (rb[step - 2, yy].astype(F32) + own).astype(BF16)
                gb[step, yy] = remote(sb.at[step - 2, yy], rb.at[step - 1, yy], z_bwd)

    if LA > 2:
        for d in range(NY):
            w_recv(LA, d)

    for yy in range(NY):
        k_part[:, yy * kb : (yy + 1) * kb] = lax.dot_general(
            norm[...],
            wall[yy].reshape(kb, half),
            (((1,), (1,)), ((), ())),
            preferred_element_type=F32,
        )
    kc_s[...] = k_part[pl.ds(pl.multiple_of((1 - c) * rows, rows), rows), :]
    r_kc = remote(kc_s, kc_r, partner)

    gain_sum = jnp.zeros((1, half), F32)
    for yy in range(NY):
        gain_sum += jnp.sum(
            (gf[yy] * wall[yy].astype(F32)).reshape(kb, half), axis=0, keepdims=True
        )
    gz[pl.ds(z, 1)] = gain_sum[None]
    r_gz = [
        remote(gz.at[z], gz.at[z], at_dp(y, lax.rem(z + d, NZ), c)) for d in range(1, NZ)
    ]

    r_kc.wait_recv()
    own_k = k_part[pl.ds(pl.multiple_of(c * rows, rows), rows), :] + kc_r[...]
    for q in range(NX):
        kx_s[q] = own_k[:, q * qcols : (q + 1) * qcols].astype(BF16)
    kx_r[pl.ds(x, 1)] = kx_s[pl.ds(x, 1)]
    r_kx = []
    for d in range(1, NX):
        xx = lax.rem(x + d, NX)
        r_kx.append(remote(kx_s.at[xx], kx_r.at[x], {"tensor": h * NX + xx}))

    if LA >= 2:
        g_step(2)

    recv(r_kx)
    mine_k = kx_r[0].astype(F32)
    for q in range(1, NX):
        mine_k = mine_k + kx_r[q].astype(F32)
    if NH == 2:
        kh_s[...] = mine_k.astype(BF16)
        r_kh = remote(kh_s, kh_r, {"tensor": (1 - h) * NX + x})

    recv(r_gz)
    gain_sum = gz[0]
    for i in range(1, NZ):
        gain_sum = gain_sum + gz[i]
    gyb[pl.ds(y, 1)] = gain_sum[None]
    r_gy = [
        remote(gyb.at[y], gyb.at[y], at_dp(lax.rem(y + d, NY), z, c)) for d in range(1, NY)
    ]

    if LA >= 3:
        g_step(3)

    if NH == 2:
        r_kh.wait_recv()
        mine_k = kh_s[...].astype(F32) + kh_r[...].astype(F32)
    r_yc = (drow // (2 * NZ)) * 2 + drow % 2
    r_z = (drow // 2) % NZ
    pos_row = r_z * (4 * NY) + r_yc * 2 + rank_row
    place = onehot(
        (iota((slots, rows), 0) == pos_row) & (iota((slots, rows), 1) < count)
    )
    kz_s[...] = dot(place, mine_k.astype(BF16)).astype(BF16).reshape(NZ, 4 * NY, qcols)
    r_kz = z_exchange(kz_s, kz_r)
    kz_r[pl.ds(z, 1)] = kz_s[pl.ds(z, 1)]

    for step in range(4, LA + 1):
        g_step(step)

    recv(r_gy)
    gain_sum = gyb[0]
    for i in range(1, NY):
        gain_sum = gain_sum + gyb[i]
    gcb[pl.ds(c, 1)] = (gain_sum * factor / gain_half)[None]
    r_gc = remote(gcb.at[c], gcb.at[c], partner)

    recv(r_kz)
    ky_s[...] = (
        dot(perm_yz(), kz_r[...].reshape(slots, qcols)).astype(BF16).reshape(2 * NY, 2 * NZ, qcols)
    )
    r_ky = yc_exchange(ky_s, ky_r)
    ky_r[pl.ds(y * 2 + c, 1)] = ky_s[pl.ds(y * 2 + c, 1)]

    summed = []
    for yy in range(NY):
        ga[LA, yy].wait_recv()
        acc = gf[yy, pl.ds(z, 1)][0] + ra[LA - 1, yy].astype(F32)
        if LB:
            gb[LB, yy].wait_recv()
            acc = acc + rb[LB - 1, yy].astype(F32)
        gy_s[yy] = acc.astype(BF16)
    r_gyx = []
    for d in range(1, NY):
        yy = lax.rem(y + d, NY)
        r_gyx.append(remote(gy_s.at[yy], gy_r.at[y], at_dp(yy, z, c)))
    gy_r[pl.ds(y, 1)] = gy_s[pl.ds(y, 1)]

    recv(r_ky)
    kout[pl.ds(x, 1)] = (
        dot(perm_out(), ky_r[...].reshape(slots, qcols)).astype(BF16)[None]
    )
    r_ko = []
    for d in range(1, NX):
        r_ko.append(remote(kout.at[x], kout.at[x], {"tensor": h * NX + lax.rem(x + d, NX)}))

    recv(r_gyx)
    acc = gy_r[0].astype(F32)
    for i in range(1, NY):
        acc = acc + gy_r[i].astype(F32)
    acc = acc * factor
    low, high = acc[: acc.shape[0] // 2], acc[acc.shape[0] // 2 :]
    gc_s[...] = jnp.where(c == 0, high, low)
    r_gcx = remote(gc_s, gout.at[c], partner)
    gout[pl.ds(c, 1)] = jnp.where(c == 0, low, high)[None]

    r_gc.wait_recv()
    outs = [local(gcb.at[i], gg_out.at[:, i * half : (i + 1) * half]) for i in range(2)]
    r_gcx.wait_recv()
    outs += [local(gout.at[i], gw_out.at[:, i * half : (i + 1) * half]) for i in range(2)]
    recv(r_ko)
    outs += [
        local(kout.at[q], keys_out.at[0, :, q * qcols : (q + 1) * qcols]) for q in range(NX)
    ]
    for d in sends:
        d.wait_send()
    for d in outs:
        d.wait()


def build(mesh, dims):
    NY, NZ, NH, NX = dims
    LA, LB = NZ // 2, NZ // 2 - 1

    def on_device(hidden_rows, norm_gain, key_weight, cotangent, accepted_counts, destination):
        rows, cols = hidden_rows.shape
        half = cols // 2
        kvw = cotangent.shape[2]
        slots = 2 * rows
        kr = key_weight.shape[0]
        qcols = kvw // NX
        factor = 1.0 / math.sqrt(rows * lax.axis_size("dp"))
        V = pltpu.VMEM
        ncopies = 200
        scratch = [
            V((2, rows, half), BF16),
            V((kr, half), BF16),
            V((kr, half), BF16),
            V((NY, NZ, 2 * kr, half), BF16),
            V((slots, kvw), BF16),
            V((NZ, 4 * NY, kvw), BF16),
            V((NZ, 4 * NY, kvw), BF16),
            V((2 * NY, 2 * NZ, kvw), BF16),
            V((2 * NY, 2 * NZ, kvw), BF16),
            V((2, rows, kvw), BF16),
            V((NH * NX, 1, 2 * rows), F32),
            V((2, 1, 2 * rows), F32),
            V((2 * rows, half), BF16),
            V((NY, NZ, 2 * kr, half), F32),
            V((NY, NZ, 2 * kr, half), BF16),
            V((LA, NY, 2 * kr, half), BF16),
            V((max(LB, 1), NY, 2 * kr, half), BF16),
            V((max(LA - 1, 1), NY, 2 * kr, half), BF16),
            V((max(LB - 1, 1), NY, 2 * kr, half), BF16),
            V((NY, 2 * kr, half), BF16),
            V((NY, 2 * kr, half), BF16),
            V((kr, half), F32),
            V((2, kr, half), F32),
            V((NZ, 1, half), F32),
            V((NY, 1, half), F32),
            V((2, 1, half), F32),
            V((2 * rows, kvw), F32),
            V((rows, kvw), F32),
            V((rows, kvw), F32),
            V((NX, rows, qcols), BF16),
            V((NX, rows, qcols), BF16),
            V((rows, qcols), BF16),
            V((rows, qcols), BF16),
            V((NZ, 4 * NY, qcols), BF16),
            V((NZ, 4 * NY, qcols), BF16),
            V((2 * NY, 2 * NZ, qcols), BF16),
            V((2 * NY, 2 * NZ, qcols), BF16),
            V((NX, slots, qcols), BF16),
            pltpu.SemaphoreType.DMA((ncopies,)),
            pltpu.SemaphoreType.DMA((ncopies,)),
            pltpu.SemaphoreType.DMA((16,)),
        ]
        any_spec = pl.BlockSpec(memory_space=pl.ANY)
        vmem = pl.BlockSpec(memory_space=pltpu.VMEM)
        smem = pl.BlockSpec(memory_space=pltpu.SMEM)
        keys, gw, gg = pl.pallas_call(
            functools.partial(kernel, dims, factor),
            out_shape=(
                jax.ShapeDtypeStruct((1, slots, kvw), BF16),
                jax.ShapeDtypeStruct((kr, cols), F32),
                jax.ShapeDtypeStruct((1, cols), F32),
            ),
            in_specs=[any_spec, vmem, any_spec, any_spec, smem, vmem],
            out_specs=(any_spec, any_spec, any_spec),
            scratch_shapes=scratch,
            compiler_params=pltpu.CompilerParams(collective_id=0, has_side_effects=True),
        )(
            hidden_rows,
            norm_gain.reshape(1, cols),
            key_weight,
            cotangent,
            accepted_counts,
            destination.reshape(1, rows),
        )
        return keys, gw, gg.reshape(cols)

    return jax.shard_map(
        on_device,
        mesh=mesh,
        in_specs=(
            P("dp", "tensor"),
            P("tensor"),
            P("dp", "tensor"),
            P("dp", None, None),
            P("dp"),
            P("dp"),
        ),
        out_specs=(P("dp", None, None), P("dp", "tensor"), P("tensor")),
        check_vma=False,
    )


def solution(mesh):
    return build(mesh, (4, 8, 2, 4))
```

time: 437 us -> 66.8 us (0.15); the launches traced: 432 us -> 66.6 us
  blocking collectives: 242 us -> 0 us
  waiting for transfers between devices: 153 us -> 0 us
  Pallas kernels: 0 us -> 62.4 us
  between operations: 14.8 us -> 1.3 us
  local copies, waits for them, and re-layouts: 11.1 us -> 2.9 us
  matrix products: 5.84 us -> 0 us
    psum x3 -> x0, blocking collectives: 209 us -> none  [the longest x1 135 us: on_device(): grad_gain = lax.psum(gain_term, 'dp') * factor / norm_gain]
    unnamed x3 -> x0, waiting for transfers between devices: 96.3 us -> none
    pallas_call x0 -> x1, Pallas kernels: none -> 62.4 us  [on_device(): pl.pallas_call(functools.partial(kernel, dims, factor), out_shape=(jax.Sh...]
    all_gather x1 -> x0, waiting for transfers between devices: 57.2 us -> none  [on_device(): weights_whole = lax.all_gather(key_weight, 'dp', axis=0, tiled=True)]
    all_to_all x1 -> x0, blocking collectives: 33.1 us -> none  [on_device(): lax.all_to_all(with_blank(hidden_rows)[filler], 'dp', split_axis=0, conca...]
    dot_general x3 -> x0, matrix products: 5.84 us -> none  [the longest x1 2.7 us: on_device(): lax.dot_general(row_cot, normed, (((0,), (0,)), ((), ())), preferred_elem...]
    unnamed x9 -> x7, local copies, waits for them, and re-layouts: 7.5 us -> 2.9 us
  transfers between devices with their start and end apart: 2 -> 0, of which waited for: 2 -> 0; matrix products, arithmetic and copies ran while one was open for 4% -> 0% of each run, Pallas kernels for 0% -> 0%
where the time goes in v1:
time: 66.8 us; the launch traced here: 66.6 us
  Pallas kernels  62.4 us (93%)
  local copies, waits for them, and re-layouts  2.9 us (4%)
  between operations  1.3 us (2%)
    pallas_call x1, Pallas kernels, on_device(): pl.pallas_call(functools.partial(kernel, dims, factor), out_shape=(jax.Sh...  62.4 us
    unnamed x7, local copies, waits for them, and re-layouts  2.9 us

profile of v1, /device:TPU:1, one launch (start us, length us, event | category | flops | bytes accessed | tf_op | source)
XLA Modules:
  0.0 66.6 jit_solution(14795156426821974423)
XLA Ops:
  1.3 62.4 %shard_map.85 = (bf16[1,128,512]{2,1,0:T(8,128)(2,1)}, f32[8,2048]{1,0:T(8,128)}, f32[1,2048]{1,0:T(1,128)}) custom-call(bf16[64,2048]{1,0:T(8,128)(2,1)} %hid.1, f32[1,2048]{1,0:T(1,128)} %bitcast.3, bf16[8,2048]{1,0:T(8,128)(2,1)} %wsh.1, bf16[1,128,512]{2,1,0:T(8,128)(2,1)} %cot.1, s32[1]{0:T(128)S(6)} %copy.12.count_ref, s32[1,64]{1,0:T(1,128)} %bitcast.5), custom_call_target="tpu_custom_call" | custom-call | tf_op jit(solution)/shard_map/pallas_call | solution.py:541
  63.6 0.0 copy-start
  63.7 1.6 %copy.13 = bf16[1,128,512]{2,1,0:T(8,128)(2,1)} copy(bf16[1,128,512]{2,1,0:T(8,128)(2,1)} %get-tuple-element.12) | data formatting | bytes 262144
  65.3 0.0 copy-done
  65.3 0.0 copy-start.1
  65.3 0.6 copy.14
  65.9 0.1 copy-done.1
  66.0 0.6 copy.15
Async XLA Ops:
  63.6 1.6 %copy-start = (f32[8,2048]{1,0:T(8,128)S(1)}, f32[8,2048]{1,0:T(8,128)}, u32[]{:S(2)}) copy-start(f32[8,2048]{1,0:T(8,128)} %get-tuple-element.13) | copy-start | bytes 196612
  65.3 0.7 %copy-start.1 = (f32[1,2048]{1,0:T(1,128)S(1)}, f32[1,2048]{1,0:T(1,128)}, u32[]{:S(2)}) copy-start(f32[1,2048]{1,0:T(1,128)} %get-tuple-element.8) | copy-start | bytes 24580

commit v2 on v1

v2 whole, which is shorter than its diff:
```python
import functools
import math

import jax
import jax.numpy as jnp
from jax import lax
from jax.experimental import pallas as pl
from jax.experimental.pallas import tpu as pltpu
from jax.sharding import PartitionSpec as P

EPSILON = 1e-05
F32 = jnp.float32
BF16 = jnp.bfloat16
MESH = pl.DeviceIdType.MESH


def iota(shape, dim):
    return lax.broadcasted_iota(jnp.int32, shape, dim)


def onehot(cond):
    return jnp.where(cond, 1.0, 0.0).astype(BF16)


def kernel(
    dims,
    factor,
    hid,
    gain_ref,
    wsh,
    cot,
    count_ref,
    dest_ref,
    keys_out,
    gw_out,
    gg_out,
    hown,
    hbuf,
    wall,
    permz,
    permo,
    pick,
    place,
    cotv,
    cot_a,
    cot_b1,
    cot_s,
    cot_b2,
    cot_r,
    sqb,
    sqc,
    norm,
    gf,
    gs,
    ra,
    rb,
    sa,
    sb,
    gy_s,
    gy_r,
    gc_s,
    gout,
    gz,
    gyb,
    gcb,
    k_part,
    kx_s,
    kx_r,
    kz_s,
    kz_r,
    ky_s,
    ky_r,
    kout,
    ssem,
    rsem,
    lsem,
):
    NY, NZ, NH, NX = dims
    NT = NH * NX
    dp = lax.axis_index("dp")
    t = lax.axis_index("tensor")
    c = lax.rem(dp, 2)
    z = lax.rem(lax.div(dp, 2), NZ)
    y = lax.div(dp, 2 * NZ)
    x = lax.rem(t, NX)
    h = lax.div(t, NX)
    rows = dest_ref.shape[1]
    slots = 2 * rows
    half = hbuf.shape[2]
    width = half * 2 * NT
    kvw = cotv.shape[1]
    qcols = kvw // NX
    sign = 1 - 2 * c
    LA, LB = NZ // 2, NZ // 2 - 1

    def at_dp(yy, zz, cc):
        return {"dp": (yy * NZ + zz) * 2 + cc}

    partner = at_dp(y, z, 1 - c)
    z_fwd = at_dp(y, lax.rem(z + sign + NZ, NZ), c)
    z_bwd = at_dp(y, lax.rem(z - sign + NZ, NZ), c)

    def zmod(v):
        return lax.rem(v + 2 * NZ, NZ)

    counter = [0]
    sends = []

    def remote(src, dst, dev):
        i = counter[0]
        counter[0] += 1
        d = pltpu.make_async_remote_copy(
            src_ref=src,
            dst_ref=dst,
            send_sem=ssem.at[i],
            recv_sem=rsem.at[i],
            device_id=dev,
            device_id_type=MESH,
        )
        d.start()
        sends.append(d)
        return d

    lcount = [0]

    def local(src, dst):
        i = lcount[0]
        lcount[0] += 1
        d = pltpu.make_async_copy(src, dst, lsem.at[i])
        d.start()
        return d

    own_cols = pl.ds(pl.multiple_of(c * half, half), half)
    other_cols = pl.ds(pl.multiple_of((1 - c) * half, half), half)

    barrier = pltpu.get_barrier_semaphore()
    peers = []
    for d in range(1, NZ):
        peers.append(at_dp(y, lax.rem(z + d, NZ), c))
    for dy in range(NY):
        for dc in range(2):
            if dy or dc:
                peers.append(at_dp(lax.rem(y + dy, NY), z, lax.rem(c + dc, 2)))
    for d in range(1, NT):
        peers.append({"tensor": lax.rem(t + d, NT)})
    for d in range(1, NX):
        peers.append(dict(at_dp(y, z, 1 - c), tensor=h * NX + lax.rem(x + d, NX)))
    for dy in range(NY):
        for dc in range(2):
            for dh in range(1, NH):
                if dy or dc:
                    peers.append(
                        dict(
                            at_dp(lax.rem(y + dy, NY), z, lax.rem(c + dc, 2)),
                            tensor=lax.rem(h + dh, NH) * NX + x,
                        )
                    )
    for p in peers:
        pl.semaphore_signal(barrier, inc=1, device_id=p, device_id_type=MESH)

    l_cot = local(cot.at[0], cotv)
    l_own = local(hid, hown)
    l_w = local(wsh.at[:, own_cols], wall.at[y, z, c])
    l_h = local(hid.at[:, own_cols], hbuf.at[c])

    def perm_zy():
        b = iota((slots, slots), 1)
        bz = (b // 4) % NZ
        by = b // (4 * NZ)
        return onehot(iota((slots, slots), 0) == bz * (4 * NY) + by * 4 + b % 4)

    def perm_yz():
        b = iota((slots, slots), 1)
        bz = b // (4 * NY)
        byc = (b // 2) % (2 * NY)
        return onehot(iota((slots, slots), 0) == byc * (2 * NZ) + bz * 2 + b % 2)

    def perm_out():
        b = iota((slots, slots), 1)
        by = b // (4 * NZ)
        bc = (b // (2 * NZ)) % 2
        bz = (b // 2) % NZ
        return onehot(iota((slots, slots), 0) == by * (4 * NZ) + bz * 4 + bc * 2 + b % 2)

    def dot(a, b):
        return jnp.dot(a, b, preferred_element_type=F32)

    l_cot.wait()
    mixed = dot(perm_zy(), cotv[...]).astype(BF16)
    cot_a[...] = mixed.reshape(NZ, 4 * NY, kvw)

    l_own.wait()
    eye = iota((rows, rows), 0) == iota((rows, rows), 1)

    def as_row(col):
        return jnp.sum(jnp.where(eye, col, 0.0), axis=0, keepdims=True)

    def as_col(row):
        return jnp.sum(jnp.where(eye, row, 0.0), axis=1, keepdims=True)

    values = hown[...].astype(F32)
    sqb[pl.ds(t, 1)] = as_row(jnp.sum(values * values, axis=1, keepdims=True))[None]

    permz[...] = perm_yz()
    permo[...] = perm_out()
    drow = dest_ref[...]
    dcol = as_col(drow.astype(F32)).astype(jnp.int32)
    same = dcol == drow
    rank_col = jnp.sum(
        jnp.where(same & (iota((rows, rows), 1) < iota((rows, rows), 0)), 1.0, 0.0),
        axis=1,
        keepdims=True,
    ).astype(jnp.int32)
    rank_row = jnp.sum(
        jnp.where(same & (iota((rows, rows), 0) < iota((rows, rows), 1)), 1.0, 0.0),
        axis=0,
        keepdims=True,
    ).astype(jnp.int32)
    count = count_ref[...]

    def yc_of(dest):
        return (dest // (2 * NZ)) * 2 + dest % 2

    def z_of(dest):
        return (dest // 2) % NZ

    pos_col = yc_of(dcol) * (2 * NZ) + z_of(dcol) * 2 + rank_col
    pick[...] = onehot((iota((rows, slots), 1) == pos_col) & (iota((rows, slots), 0) < count))
    pos_row = z_of(drow) * (4 * NY) + yc_of(drow) * 2 + rank_row
    place[...] = onehot((iota((slots, rows), 0) == pos_row) & (iota((slots, rows), 1) < count))

    pl.semaphore_wait(barrier, len(peers))

    r_wy = {}
    for d in range(NY):
        for dc in range(2):
            if d or dc:
                cc = lax.rem(c + dc, 2)
                r_wy[d, dc] = remote(
                    wsh.at[:, other_cols if dc else own_cols],
                    wall.at[y, z, c],
                    at_dp(lax.rem(y + d, NY), z, cc),
                )

    def z_exchange(src, dst):
        return [
            remote(src.at[lax.rem(z + d, NZ)], dst.at[z], at_dp(y, lax.rem(z + d, NZ), c))
            for d in range(1, NZ)
        ]

    def yc_exchange(src, dst):
        out = []
        for dy in range(NY):
            for dc in range(2):
                if dy or dc:
                    yy, cc = lax.rem(y + dy, NY), lax.rem(c + dc, 2)
                    out.append(remote(src.at[yy * 2 + cc], dst.at[y * 2 + c], at_dp(yy, z, cc)))
        return out

    def recv(copies):
        for d in copies:
            d.wait_recv()

    r_cz = z_exchange(cot_a, cot_b1)
    cot_b1[pl.ds(z, 1)] = cot_a[pl.ds(z, 1)]
    r_sq = [
        remote(sqb.at[t], sqb.at[t], {"tensor": lax.rem(t + d, NT)}) for d in range(1, NT)
    ]
    r_h = remote(hid.at[:, other_cols], hbuf.at[c], partner)

    def w_send(step, d, fwd):
        yy = lax.rem(y - d + NY, NY)
        zz = zmod(z - (step - 1) * sign) if fwd else zmod(z + (step - 1) * sign)
        return remote(wall.at[yy, zz], wall.at[yy, zz], z_fwd if fwd else z_bwd)

    wa, wb = {}, {}

    def w_step(step, d):
        if step <= LA:
            wa[step, d] = w_send(step, d, True)
        if step <= LB:
            wb[step, d] = w_send(step, d, False)

    def w_recv(step, d):
        if step <= LA:
            wa[step, d].wait_recv()
        if step <= LB:
            wb[step, d].wait_recv()

    l_w.wait()
    r_wy[0, 1].wait_recv()
    w_step(1, 0)
    for d in range(1, NY):
        r_wy[d, 0].wait_recv()
        r_wy[d, 1].wait_recv()
        w_step(1, d)

    w_recv(1, 0)
    w_step(2, 0)

    recv(r_cz)
    cot_s[...] = (
        dot(permz[...], cot_b1[...].reshape(slots, kvw)).astype(BF16).reshape(2 * NY, 2 * NZ, kvw)
    )
    r_cy = yc_exchange(cot_s, cot_b2)
    cot_b2[pl.ds(y * 2 + c, 1)] = cot_s[pl.ds(y * 2 + c, 1)]

    for d in range(1, NY):
        w_recv(1, d)
        w_step(2, d)

    recv(r_sq)
    total = sqb[0]
    for i in range(1, NT):
        total = total + sqb[i]
    sqc[pl.ds(c, 1)] = total[None]
    r_sc = remote(sqc.at[c], sqc.at[c], partner)

    for d in range(NY):
        w_recv(2, d)
        w_step(3, d)

    recv(r_cy)
    cot_r[pl.ds(c, 1)] = dot(pick[...], cot_b2[...].reshape(slots, kvw)).astype(BF16)[None]
    r_cr = remote(cot_r.at[c], cot_r.at[c], partner)

    for step in range(3, LA):
        for d in range(NY):
            w_recv(step, d)
            w_step(step + 1, d)

    l_h.wait()
    r_h.wait_recv()
    r_sc.wait_recv()
    gain_half = gain_ref[:, own_cols]
    for i in range(2):
        scale = as_col(lax.rsqrt(sqc[i] / width + EPSILON))
        norm[i * rows : (i + 1) * rows] = (hbuf[i].astype(F32) * scale * gain_half).astype(BF16)

    r_cr.wait_recv()
    cot2 = cot_r[...].reshape(2 * rows, kvw)
    kb = kvw // NY
    for yy in range(NY):
        part = lax.dot_general(
            cot2[:, yy * kb : (yy + 1) * kb],
            norm[...],
            (((0,), (0,)), ((), ())),
            preferred_element_type=F32,
        ).reshape(NZ, kb // NZ, half)
        gf[yy] = part
        gs[yy] = part.astype(BF16)

    ga, gb = {}, {}
    order = list(range(1, NY)) + [0]
    za1, zb1 = zmod(z + LA * sign), zmod(z - LB * sign)

    def y_of(j):
        return lax.rem(y + j, NY)

    def own_g(j, zz):
        return gf[pl.ds(y_of(j), 1), pl.ds(zz, 1)][0, 0]

    for j in order:
        ga[1, j] = remote(gs.at[y_of(j), za1], ra.at[0, j], z_fwd)
        if LB:
            gb[1, j] = remote(gs.at[y_of(j), zb1], rb.at[0, j], z_bwd)

    def g_step(step):
        for j in order:
            if step <= LA:
                ga[step - 1, j].wait_recv()
                own = own_g(j, zmod(z + (LA + 1 - step) * sign))
                sa[step - 2, j] = (ra[step - 2, j].astype(F32) + own).astype(BF16)
                ga[step, j] = remote(sa.at[step - 2, j], ra.at[step - 1, j], z_fwd)
            if step <= LB:
                gb[step - 1, j].wait_recv()
                own = own_g(j, zmod(z - (LB + 1 - step) * sign))
                sb[step - 2, j] = (rb[step - 2, j].astype(F32) + own).astype(BF16)
                gb[step, j] = remote(sb.at[step - 2, j], rb.at[step - 1, j], z_bwd)

    if LA > 2:
        for d in range(NY):
            w_recv(LA, d)

    for yy in range(NY):
        k_part[:, yy * kb : (yy + 1) * kb] = lax.dot_general(
            norm[...],
            wall[yy].reshape(kb, half),
            (((1,), (1,)), ((), ())),
            preferred_element_type=F32,
        )
    for q in range(NX):
        block = k_part[:, q * qcols : (q + 1) * qcols].astype(BF16)
        kx_s[q] = block.reshape(2, rows, qcols)
    r_kx = []
    for dc in range(2):
        for d in range(NX):
            if d or dc:
                xx, cc = lax.rem(x + d, NX), lax.rem(c + dc, 2)
                r_kx.append(
                    remote(
                        kx_s.at[xx, cc],
                        kx_r.at[x, c],
                        dict(at_dp(y, z, cc), tensor=h * NX + xx),
                    )
                )
    kx_r[pl.ds(x, 1), pl.ds(c, 1)] = kx_s[pl.ds(x, 1), pl.ds(c, 1)]

    gain_sum = jnp.zeros((1, half), F32)
    for yy in range(NY):
        gain_sum += jnp.sum(
            gf[yy].reshape(kb, half) * wall[yy].reshape(kb, half).astype(F32), axis=0, keepdims=True
        )
    gz[pl.ds(z, 1)] = gain_sum[None]
    r_gz = [
        remote(gz.at[z], gz.at[z], at_dp(y, lax.rem(z + d, NZ), c)) for d in range(1, NZ)
    ]

    if LA >= 2:
        g_step(2)

    recv(r_kx)
    mine_k = kx_r[0, 0].astype(F32)
    for i in range(1, 2 * NX):
        mine_k = mine_k + kx_r[i // 2, i % 2].astype(F32)
    kz_s[...] = dot(place[...], mine_k.astype(BF16)).astype(BF16).reshape(NZ, 4 * NY, qcols)
    r_kz = z_exchange(kz_s, kz_r)
    kz_r[pl.ds(z, 1)] = kz_s[pl.ds(z, 1)]

    recv(r_gz)
    gain_sum = gz[0]
    for i in range(1, NZ):
        gain_sum = gain_sum + gz[i]
    gyb[pl.ds(y, 1)] = gain_sum[None]
    r_gy = [
        remote(gyb.at[y], gyb.at[y], at_dp(lax.rem(y + d, NY), z, c)) for d in range(1, NY)
    ]

    if LA >= 3:
        g_step(3)

    for step in range(4, LA + 1):
        g_step(step)

    recv(r_gy)
    gain_sum = gyb[0]
    for i in range(1, NY):
        gain_sum = gain_sum + gyb[i]
    gcb[pl.ds(c, 1)] = (gain_sum * factor / gain_half)[None]
    r_gc = remote(gcb.at[c], gcb.at[c], partner)

    recv(r_kz)
    ky_s[...] = (
        dot(permz[...], kz_r[...].reshape(slots, qcols)).astype(BF16).reshape(2 * NY, 2 * NZ, qcols)
    )
    r_ky = []
    for dh in range(NH):
        for dy in range(NY):
            for dc in range(2):
                if dy or dc or dh:
                    yy, cc, hh = lax.rem(y + dy, NY), lax.rem(c + dc, 2), lax.rem(h + dh, NH)
                    r_ky.append(
                        remote(
                            ky_s.at[yy * 2 + cc],
                            ky_r.at[h, y * 2 + c],
                            dict(at_dp(yy, z, cc), tensor=hh * NX + x),
                        )
                    )
    ky_r[pl.ds(h, 1), pl.ds(y * 2 + c, 1)] = ky_s[pl.ds(y * 2 + c, 1)][None]

    r_gyx = []
    for j in order:
        ga[LA, j].wait_recv()
        acc = own_g(j, z) + ra[LA - 1, j].astype(F32)
        if LB:
            gb[LB, j].wait_recv()
            acc = acc + rb[LB - 1, j].astype(F32)
        if j:
            gy_s[j] = acc.astype(BF16)
            r_gyx.append(remote(gy_s.at[j], gy_r.at[j], at_dp(y_of(j), z, c)))

    recv(r_ky)
    whole = ky_r[0].astype(F32)
    for i in range(1, NH):
        whole = whole + ky_r[i].astype(F32)
    kout[pl.ds(x, 1)] = (
        dot(permo[...], whole.astype(BF16).reshape(slots, qcols)).astype(BF16)[None]
    )
    r_ko = []
    for d in range(1, NX):
        r_ko.append(remote(kout.at[x], kout.at[x], {"tensor": h * NX + lax.rem(x + d, NX)}))

    recv(r_gyx)
    for i in range(1, NY):
        acc = acc + gy_r[i].astype(F32)
    acc = acc * factor
    low, high = acc[: acc.shape[0] // 2], acc[acc.shape[0] // 2 :]
    gc_s[...] = jnp.where(c == 0, high, low)
    r_gcx = remote(gc_s, gout.at[c], partner)
    gout[pl.ds(c, 1)] = jnp.where(c == 0, low, high)[None]

    r_gc.wait_recv()
    outs = [local(gcb.at[i], gg_out.at[:, i * half : (i + 1) * half]) for i in range(2)]
    r_gcx.wait_recv()
    outs += [local(gout.at[i], gw_out.at[:, i * half : (i + 1) * half]) for i in range(2)]
    recv(r_ko)
    outs += [
        local(kout.at[q], keys_out.at[0, :, q * qcols : (q + 1) * qcols]) for q in range(NX)
    ]
    for d in sends:
        d.wait_send()
    for d in outs:
        d.wait()


def write_out(k_in, gw_in, gg_in, k_out, gw_out, gg_out, sem):
    pairs = ((k_in, k_out), (gw_in, gw_out), (gg_in, gg_out))
    copies = [pltpu.make_async_copy(a, b, sem.at[i]) for i, (a, b) in enumerate(pairs)]
    for d in copies:
        d.start()
    for d in copies:
        d.wait()


def build(mesh, dims):
    NY, NZ, NH, NX = dims
    LA, LB = NZ // 2, NZ // 2 - 1

    def on_device(hidden_rows, norm_gain, key_weight, cotangent, accepted_counts, destination):
        rows, cols = hidden_rows.shape
        half = cols // 2
        kvw = cotangent.shape[2]
        slots = 2 * rows
        kr = key_weight.shape[0]
        qcols = kvw // NX
        factor = 1.0 / math.sqrt(rows * lax.axis_size("dp"))
        V = pltpu.VMEM
        ncopies = 200
        scratch = [
            V((rows, cols), BF16),
            V((2, rows, half), BF16),
            V((NY, NZ, 2, kr, half), BF16),
            V((slots, slots), BF16),
            V((slots, slots), BF16),
            V((rows, slots), BF16),
            V((slots, rows), BF16),
            V((slots, kvw), BF16),
            V((NZ, 4 * NY, kvw), BF16),
            V((NZ, 4 * NY, kvw), BF16),
            V((2 * NY, 2 * NZ, kvw), BF16),
            V((2 * NY, 2 * NZ, kvw), BF16),
            V((2, rows, kvw), BF16),
            V((NH * NX, 1, rows), F32),
            V((2, 1, rows), F32),
            V((2 * rows, half), BF16),
            V((NY, NZ, 2 * kr, half), F32),
            V((NY, NZ, 2 * kr, half), BF16),
            V((LA, NY, 2 * kr, half), BF16),
            V((max(LB, 1), NY, 2 * kr, half), BF16),
            V((max(LA - 1, 1), NY, 2 * kr, half), BF16),
            V((max(LB - 1, 1), NY, 2 * kr, half), BF16),
            V((NY, 2 * kr, half), BF16),
            V((NY, 2 * kr, half), BF16),
            V((kr, half), F32),
            V((2, kr, half), F32),
            V((NZ, 1, half), F32),
            V((NY, 1, half), F32),
            V((2, 1, half), F32),
            V((2 * rows, kvw), F32),
            V((NX, 2, rows, qcols), BF16),
            V((NX, 2, rows, qcols), BF16),
            V((NZ, 4 * NY, qcols), BF16),
            V((NZ, 4 * NY, qcols), BF16),
            V((2 * NY, 2 * NZ, qcols), BF16),
            V((NH, 2 * NY, 2 * NZ, qcols), BF16),
            V((NX, slots, qcols), BF16),
            pltpu.SemaphoreType.DMA((ncopies,)),
            pltpu.SemaphoreType.DMA((ncopies,)),
            pltpu.SemaphoreType.DMA((16,)),
        ]
        any_spec = pl.BlockSpec(memory_space=pl.ANY)
        vmem = pl.BlockSpec(memory_space=pltpu.VMEM)
        keys, gw, gg = pl.pallas_call(
            functools.partial(kernel, dims, factor),
            out_shape=(
                jax.ShapeDtypeStruct((1, slots, kvw), BF16),
                jax.ShapeDtypeStruct((kr, cols), F32),
                jax.ShapeDtypeStruct((1, cols), F32),
            ),
            in_specs=[any_spec, vmem, any_spec, any_spec, vmem, vmem],
            out_specs=(vmem, vmem, vmem),
            scratch_shapes=scratch,
            compiler_params=pltpu.CompilerParams(collective_id=0, has_side_effects=True),
            name="exchange",
        )(
            hidden_rows,
            norm_gain.reshape(1, cols),
            key_weight,
            cotangent,
            accepted_counts.reshape(1, 1),
            destination.reshape(1, rows),
        )
        keys, gw, gg = pl.pallas_call(
            write_out,
            out_shape=tuple(jax.ShapeDtypeStruct(a.shape, a.dtype) for a in (keys, gw, gg)),
            in_specs=[vmem] * 3,
            out_specs=(any_spec,) * 3,
            scratch_shapes=[pltpu.SemaphoreType.DMA((3,))],
            name="results",
        )(keys, gw, gg)
        return keys, gw, gg.reshape(cols)

    return jax.shard_map(
        on_device,
        mesh=mesh,
        in_specs=(
            P("dp", "tensor"),
            P("tensor"),
            P("dp", "tensor"),
            P("dp", None, None),
            P("dp"),
            P("dp"),
        ),
        out_specs=(P("dp", None, None), P("dp", "tensor"), P("tensor")),
        check_vma=False,
    )


def solution(mesh):
    return build(mesh, (4, 8, 2, 4))
```

time: 66.8 us -> 62.6 us (0.937)
  local copies, waits for them, and re-layouts: 2.9 us -> 0 us
  Pallas kernels: 62.4 us -> 61.1 us
    pallas_call x1, Pallas kernels: 62.4 us -> 59.4 us  [on_device(): pl.pallas_call(functools.partial(kernel, dims, factor), out_shape=(jax.Sh...]
    unnamed x7 -> x0, local copies, waits for them, and re-layouts: 2.9 us -> none
    pallas_call x0 -> x1, Pallas kernels: none -> 1.65 us  [on_device(): pl.pallas_call(write_out, out_shape=tuple((jax.ShapeDtypeStruct(a.shape,...]
where the time goes in v2:
time: 62.6 us; the launch traced here: 62.4 us
  Pallas kernels  61.1 us (98%)
  between operations  1.29 us (2%)
    pallas_call x1, Pallas kernels, on_device(): pl.pallas_call(functools.partial(kernel, dims, factor), out_shape=(jax.Sh...  59.4 us
    pallas_call x1, Pallas kernels, on_device(): pl.pallas_call(write_out, out_shape=tuple((jax.ShapeDtypeStruct(a.shape,...  1.65 us

profile of v2, /device:TPU:1, one launch (start us, length us, event | category | flops | bytes accessed | tf_op | source)
XLA Modules:
  0.0 62.4 jit_solution(8391291562819320123)
XLA Ops:
  1.3 59.4 %exchange.1 = (bf16[1,128,512]{2,1,0:T(8,128)(2,1)}, f32[8,2048]{1,0:T(8,128)}, f32[1,2048]{1,0:T(1,128)}) custom-call(bf16[64,2048]{1,0:T(8,128)(2,1)} %hid.1, f32[1,2048]{1,0:T(1,128)} %bitcast.5, bf16[8,2048]{1,0:T(8,128)(2,1)} %wsh.1, bf16[1,128,512]{2,1,0:T(8,128)(2,1)} %cot.1, s32[1,1]{1,0:T(1,128)} %bitcast.4.count_ref, s32[1,64]{1,0:T(1,128)} %bitcast.6), custom_call_target="tpu_custom_call" | custom-call | tf_op jit(solution)/shard_map/exchange/pallas_call | solution.py:583
  60.7 1.6 %results.1 = (bf16[1,128,512]{2,1,0:T(8,128)(2,1)}, f32[8,2048]{1,0:T(8,128)}, f32[1,2048]{1,0:T(1,128)}) custom-call(bf16[1,128,512]{2,1,0:T(8,128)(2,1)} %get-tuple-element.9.k_in, f32[8,2048]{1,0:T(8,128)} %get-tuple-element.10.gw_in, f32[1,2048]{1,0:T(1,128)} %get-tuple-element.11.gg_in), custom_call_target="tpu_custom_call" | custom-call | tf_op jit(solution)/shard_map/results/pallas_call | solution.py:603

commit v3 on v2

--- a/solution.py
+++ b/solution.py
@@ -35,6 +35,7 @@
     gw_out,
     gg_out,
     hown,
+    wown,
     hbuf,
     wall,
     permz,
@@ -52,6 +53,7 @@
     norm,
     gf,
     gs,
+    rj,
     ra,
     rb,
     sa,
@@ -63,7 +65,6 @@
     gz,
     gyb,
     gcb,
-    k_part,
     kx_s,
     kx_r,
     kz_s,
@@ -99,6 +100,7 @@
     partner = at_dp(y, z, 1 - c)
     z_fwd = at_dp(y, lax.rem(z + sign + NZ, NZ), c)
     z_bwd = at_dp(y, lax.rem(z - sign + NZ, NZ), c)
+    z_jump = at_dp(y, lax.rem(z + 2 * sign + NZ, NZ), c)
 
     def zmod(v):
         return lax.rem(v + 2 * NZ, NZ)
@@ -160,6 +162,7 @@
 
     l_cot = local(cot.at[0], cotv)
     l_own = local(hid, hown)
+    l_wv = local(wsh, wown)
     l_w = local(wsh.at[:, own_cols], wall.at[y, z, c])
     l_h = local(hid.at[:, own_cols], hbuf.at[c])
 
@@ -229,6 +232,7 @@
     pos_row = z_of(drow) * (4 * NY) + yc_of(drow) * 2 + rank_row
     place[...] = onehot((iota((slots, rows), 0) == pos_row) & (iota((slots, rows), 1) < count))
 
+    l_wv.wait()
     pl.semaphore_wait(barrier, len(peers))
 
     r_wy = {}
@@ -237,7 +241,7 @@
             if d or dc:
                 cc = lax.rem(c + dc, 2)
                 r_wy[d, dc] = remote(
-                    wsh.at[:, other_cols if dc else own_cols],
+                    wown.at[:, other_cols if dc else own_cols],
                     wall.at[y, z, c],
                     at_dp(lax.rem(y + d, NY), z, cc),
                 )
@@ -266,26 +270,24 @@
     r_sq = [
         remote(sqb.at[t], sqb.at[t], {"tensor": lax.rem(t + d, NT)}) for d in range(1, NT)
     ]
-    r_h = remote(hid.at[:, other_cols], hbuf.at[c], partner)
-
-    def w_send(step, d, fwd):
+    r_h = remote(hown.at[:, other_cols], hbuf.at[c], partner)
+
+    def w_send(step, d, fwd, to):
         yy = lax.rem(y - d + NY, NY)
         zz = zmod(z - (step - 1) * sign) if fwd else zmod(z + (step - 1) * sign)
-        return remote(wall.at[yy, zz], wall.at[yy, zz], z_fwd if fwd else z_bwd)
-
-    wa, wb = {}, {}
+        return remote(wall.at[yy, zz], wall.at[yy, zz], to)
+
+    w_got = {}
 
     def w_step(step, d):
-        if step <= LA:
-            wa[step, d] = w_send(step, d, True)
         if step <= LB:
-            wb[step, d] = w_send(step, d, False)
+            w_got[step, d] = [w_send(step, d, True, z_fwd), w_send(step, d, False, z_bwd)]
+        if step == LB:
+            w_got[LA, d] = [w_send(step, d, True, z_jump)]
 
     def w_recv(step, d):
-        if step <= LA:
-            wa[step, d].wait_recv()
-        if step <= LB:
-            wb[step, d].wait_recv()
+        for r in w_got.pop((step, d), ()):
+            r.wait_recv()
 
     l_w.wait()
     r_wy[0, 1].wait_recv()
@@ -323,11 +325,6 @@
     recv(r_cy)
     cot_r[pl.ds(c, 1)] = dot(pick[...], cot_b2[...].reshape(slots, kvw)).astype(BF16)[None]
     r_cr = remote(cot_r.at[c], cot_r.at[c], partner)
-
-    for step in range(3, LA):
-        for d in range(NY):
-            w_recv(step, d)
-            w_step(step + 1, d)
 
     l_h.wait()
     r_h.wait_recv()
@@ -350,9 +347,8 @@
         gf[yy] = part
         gs[yy] = part.astype(BF16)
 
-    ga, gb = {}, {}
+    ga, gb, gj = {}, {}, {}
     order = list(range(1, NY)) + [0]
-    za1, zb1 = zmod(z + LA * sign), zmod(z - LB * sign)
 
     def y_of(j):
         return lax.rem(y + j, NY)
@@ -361,37 +357,37 @@
         return gf[pl.ds(y_of(j), 1), pl.ds(zz, 1)][0, 0]
 
     for j in order:
-        ga[1, j] = remote(gs.at[y_of(j), za1], ra.at[0, j], z_fwd)
-        if LB:
-            gb[1, j] = remote(gs.at[y_of(j), zb1], rb.at[0, j], z_bwd)
+        ga[1, j] = remote(gs.at[y_of(j), zmod(z + LB * sign)], ra.at[0, j], z_fwd)
+        gb[1, j] = remote(gs.at[y_of(j), zmod(z - LB * sign)], rb.at[0, j], z_bwd)
+        gj[j] = remote(gs.at[y_of(j), zmod(z + LA * sign)], rj.at[j], z_jump)
 
     def g_step(step):
+        if step > LB:
+            return
         for j in order:
-            if step <= LA:
-                ga[step - 1, j].wait_recv()
-                own = own_g(j, zmod(z + (LA + 1 - step) * sign))
-                sa[step - 2, j] = (ra[step - 2, j].astype(F32) + own).astype(BF16)
-                ga[step, j] = remote(sa.at[step - 2, j], ra.at[step - 1, j], z_fwd)
-            if step <= LB:
-                gb[step - 1, j].wait_recv()
-                own = own_g(j, zmod(z - (LB + 1 - step) * sign))
-                sb[step - 2, j] = (rb[step - 2, j].astype(F32) + own).astype(BF16)
-                gb[step, j] = remote(sb.at[step - 2, j], rb.at[step - 1, j], z_bwd)
-
-    if LA > 2:
-        for d in range(NY):
-            w_recv(LA, d)
-
-    for yy in range(NY):
-        k_part[:, yy * kb : (yy + 1) * kb] = lax.dot_general(
+            ga[step - 1, j].wait_recv()
+            acc = ra[step - 2, j].astype(F32) + own_g(j, zmod(z + (LA - step) * sign))
+            if step == 2:
+                gj[j].wait_recv()
+                acc = acc + rj[j].astype(F32)
+            sa[step - 2, j] = acc.astype(BF16)
+            ga[step, j] = remote(sa.at[step - 2, j], ra.at[step - 1, j], z_fwd)
+            gb[step - 1, j].wait_recv()
+            acc = rb[step - 2, j].astype(F32) + own_g(j, zmod(z - (LA - step) * sign))
+            sb[step - 2, j] = acc.astype(BF16)
+            gb[step, j] = remote(sb.at[step - 2, j], rb.at[step - 1, j], z_bwd)
+
+    for d in range(NY):
+        for step in range(3, LA + 1):
+            w_recv(step, d)
+        yy = lax.rem(y - d + NY, NY)
+        block = lax.dot_general(
             norm[...],
-            wall[yy].reshape(kb, half),
+            wall[pl.ds(yy, 1)].reshape(kb, half),
             (((1,), (1,)), ((), ())),
             preferred_element_type=F32,
         )
-    for q in range(NX):
-        block = k_part[:, q * qcols : (q + 1) * qcols].astype(BF16)
-        kx_s[q] = block.reshape(2, rows, qcols)
+        kx_s[pl.ds(yy, 1)] = block.astype(BF16).reshape(1, 2, rows, qcols)
     r_kx = []
     for dc in range(2):
         for d in range(NX):
@@ -416,9 +412,6 @@
         remote(gz.at[z], gz.at[z], at_dp(y, lax.rem(z + d, NZ), c)) for d in range(1, NZ)
     ]
 
-    if LA >= 2:
-        g_step(2)
-
     recv(r_kx)
     mine_k = kx_r[0, 0].astype(F32)
     for i in range(1, 2 * NX):
@@ -426,6 +419,8 @@
     kz_s[...] = dot(place[...], mine_k.astype(BF16)).astype(BF16).reshape(NZ, 4 * NY, qcols)
     r_kz = z_exchange(kz_s, kz_r)
     kz_r[pl.ds(z, 1)] = kz_s[pl.ds(z, 1)]
+
+    g_step(2)
 
     recv(r_gz)
     gain_sum = gz[0]
@@ -435,19 +430,6 @@
     r_gy = [
         remote(gyb.at[y], gyb.at[y], at_dp(lax.rem(y + d, NY), z, c)) for d in range(1, NY)
     ]
-
-    if LA >= 3:
-        g_step(3)
-
-    for step in range(4, LA + 1):
-        g_step(step)
-
-    recv(r_gy)
-    gain_sum = gyb[0]
-    for i in range(1, NY):
-        gain_sum = gain_sum + gyb[i]
-    gcb[pl.ds(c, 1)] = (gain_sum * factor / gain_half)[None]
-    r_gc = remote(gcb.at[c], gcb.at[c], partner)
 
     recv(r_kz)
     ky_s[...] = (
@@ -468,13 +450,23 @@
                     )
     ky_r[pl.ds(h, 1), pl.ds(y * 2 + c, 1)] = ky_s[pl.ds(y * 2 + c, 1)][None]
 
+    g_step(3)
+
+    recv(r_gy)
+    gain_sum = gyb[0]
+    for i in range(1, NY):
+        gain_sum = gain_sum + gyb[i]
+    gcb[pl.ds(c, 1)] = (gain_sum * factor / gain_half)[None]
+    r_gc = remote(gcb.at[c], gcb.at[c], partner)
+
     r_gyx = []
     for j in order:
-        ga[LA, j].wait_recv()
-        acc = own_g(j, z) + ra[LA - 1, j].astype(F32)
-        if LB:
-            gb[LB, j].wait_recv()
-            acc = acc + rb[LB - 1, j].astype(F32)
+        ga[LB, j].wait_recv()
+        gb[LB, j].wait_recv()
+        acc = own_g(j, z) + ra[LB - 1, j].astype(F32) + rb[LB - 1, j].astype(F32)
+        if LB == 1:
+            gj[j].wait_recv()
+            acc = acc + rj[j].astype(F32)
         if j:
             gy_s[j] = acc.astype(BF16)
             r_gyx.append(remote(gy_s.at[j], gy_r.at[j], at_dp(y_of(j), z, c)))
@@ -538,6 +530,7 @@
         ncopies = 200
         scratch = [
             V((rows, cols), BF16),
+            V((kr, cols), BF16),
             V((2, rows, half), BF16),
             V((NY, NZ, 2, kr, half), BF16),
             V((slots, slots), BF16),
@@ -555,9 +548,10 @@
             V((2 * rows, half), BF16),
             V((NY, NZ, 2 * kr, half), F32),
             V((NY, NZ, 2 * kr, half), BF16),
-            V((LA, NY, 2 * kr, half), BF16),
-            V((max(LB, 1), NY, 2 * kr, half), BF16),
-            V((max(LA - 1, 1), NY, 2 * kr, half), BF16),
+            V((NY, 2 * kr, half), BF16),
+            V((LB, NY, 2 * kr, half), BF16),
+            V((LB, NY, 2 * kr, half), BF16),
+            V((max(LB - 1, 1), NY, 2 * kr, half), BF16),
             V((max(LB - 1, 1), NY, 2 * kr, half), BF16),
             V((NY, 2 * kr, half), BF16),
             V((NY, 2 * kr, half), BF16),
@@ -566,7 +560,6 @@
             V((NZ, 1, half), F32),
             V((NY, 1, half), F32),
             V((2, 1, half), F32),
-            V((2 * rows, kvw), F32),
             V((NX, 2, rows, qcols), BF16),
             V((NX, 2, rows, qcols), BF16),
             V((NZ, 4 * NY, qcols), BF16),
@@ -583,9 +576,9 @@
         keys, gw, gg = pl.pallas_call(
             functools.partial(kernel, dims, factor),
             out_shape=(
-                jax.ShapeDtypeStruct((1, slots, kvw), BF16),
-                jax.ShapeDtypeStruct((kr, cols), F32),
-                jax.ShapeDtypeStruct((1, cols), F32),
+                V((1, slots, kvw), BF16),
+                V((kr, cols), F32),
+                V((1, cols), F32),
             ),
             in_specs=[any_spec, vmem, any_spec, any_spec, vmem, vmem],
             out_specs=(vmem, vmem, vmem),
@@ -600,6 +593,9 @@
             accepted_counts.reshape(1, 1),
             destination.reshape(1, rows),
         )
+        keys, gw, gg = (
+            pltpu.with_memory_space_constraint(a, pltpu.VMEM) for a in (keys, gw, gg)
+        )
         keys, gw, gg = pl.pallas_call(
             write_out,
             out_shape=tuple(jax.ShapeDtypeStruct(a.shape, a.dtype) for a in (keys, gw, gg)),

time: 62.6 us -> 59.9 us (0.957)
  Pallas kernels: 61.1 us -> 58.5 us
    pallas_call x1, Pallas kernels: 59.4 us -> 57.7 us  [on_device(): pl.pallas_call(functools.partial(kernel, dims, factor), out_shape=(V((1,...]
    pallas_call x1, Pallas kernels: 1.65 us -> 0.7 us  [on_device(): pl.pallas_call(write_out, out_shape=tuple((jax.ShapeDtypeStruct(a.shape,...]
where the time goes in v3:
time: 59.9 us; the launch traced here: 59.7 us
  Pallas kernels  58.5 us (98%)
  between operations  1.29 us (2%)
    pallas_call x1, Pallas kernels, on_device(): pl.pallas_call(functools.partial(kernel, dims, factor), out_shape=(V((1,...  57.7 us

profile of v3, /device:TPU:1, one launch (start us, length us, event | category | flops | bytes accessed | tf_op | source)
XLA Modules:
  0.0 59.7 jit_solution(4136427749851871776)
XLA Ops:
  1.3 57.7 %exchange.1 = (bf16[1,128,512]{2,1,0:T(8,128)(2,1)S(1)}, f32[8,2048]{1,0:T(8,128)S(1)}, f32[1,2048]{1,0:T(1,128)S(1)}) custom-call(bf16[64,2048]{1,0:T(8,128)(2,1)} %hid.1, f32[1,2048]{1,0:T(1,128)} %bitcast.5, bf16[8,2048]{1,0:T(8,128)(2,1)} %wsh.1, bf16[1,128,512]{2,1,0:T(8,128)(2,1)} %cot.1, s32[1,1]{1,0:T(1,128)} %bitcast.4.count_ref, s32[1,64]{1,0:T(1,128)} %bitcast.6), custom_call_target="tpu_custom_call" | custom-call | tf_op jit(solution)/shard_map/exchange/pallas_call | solution.py:576
  59.0 0.7 %results.1 = (bf16[1,128,512]{2,1,0:T(8,128)(2,1)}, f32[8,2048]{1,0:T(8,128)}, f32[1,2048]{1,0:T(1,128)}) custom-call(bf16[1,128,512]{2,1,0:T(8,128)(2,1)S(1)} %get-tuple-element.9.k_in, f32[8,2048]{1,0:T(8,128)S(1)} %get-tuple-element.10.gw_in, f32[1,2048]{1,0:T(1,128)S(1)} %get-tuple-element.11.gg_in), custom_call_target="tpu_custom_call" | custom-call | tf_op jit(solution)/shard_map/results/pallas_call | solution.py:599

commit v4 on v3

--- a/solution.py
+++ b/solution.py
@@ -219,7 +219,7 @@
         axis=0,
         keepdims=True,
     ).astype(jnp.int32)
-    count = count_ref[...]
+    count = count_ref[...].reshape(1, 1)
 
     def yc_of(dest):
         return (dest // (2 * NZ)) * 2 + dest % 2
@@ -279,11 +279,19 @@
 
     w_got = {}
 
+    def w_take(step, d, i):
+        if (step, d) in w_got:
+            w_got[step, d].pop(i).wait_recv()
+
     def w_step(step, d):
         if step <= LB:
-            w_got[step, d] = [w_send(step, d, True, z_fwd), w_send(step, d, False, z_bwd)]
-        if step == LB:
-            w_got[LA, d] = [w_send(step, d, True, z_jump)]
+            w_take(step - 1, d, 0)
+            if step == LB:
+                w_got[LA, d] = [w_send(step, d, True, z_jump)]
+            w_got[step, d] = [w_send(step, d, True, z_fwd)]
+        if step <= LB:
+            w_take(step - 1, d, 0)
+            w_got[step, d].append(w_send(step, d, False, z_bwd))
 
     def w_recv(step, d):
         for r in w_got.pop((step, d), ()):
@@ -297,7 +305,6 @@
         r_wy[d, 1].wait_recv()
         w_step(1, d)
 
-    w_recv(1, 0)
     w_step(2, 0)
 
     recv(r_cz)
@@ -308,7 +315,6 @@
     cot_b2[pl.ds(y * 2 + c, 1)] = cot_s[pl.ds(y * 2 + c, 1)]
 
     for d in range(1, NY):
-        w_recv(1, d)
         w_step(2, d)
 
     recv(r_sq)
@@ -319,7 +325,6 @@
     r_sc = remote(sqc.at[c], sqc.at[c], partner)
 
     for d in range(NY):
-        w_recv(2, d)
         w_step(3, d)
 
     recv(r_cy)
@@ -378,7 +383,7 @@
             gb[step, j] = remote(sb.at[step - 2, j], rb.at[step - 1, j], z_bwd)
 
     for d in range(NY):
-        for step in range(3, LA + 1):
+        for step in range(1, LA + 1):
             w_recv(step, d)
         yy = lax.rem(y - d + NY, NY)
         block = lax.dot_general(
@@ -590,7 +595,7 @@
             norm_gain.reshape(1, cols),
             key_weight,
             cotangent,
-            accepted_counts.reshape(1, 1),
+            accepted_counts,
             destination.reshape(1, rows),
         )
         keys, gw, gg = (

time: 59.9 us -> 59 us (0.985)
  Pallas kernels: 58.5 us -> 57.5 us
    pallas_call x1, Pallas kernels: 57.7 us -> 56.8 us  [on_device(): pl.pallas_call(functools.partial(kernel, dims, factor), out_shape=(V((1,...]
where the time goes in v4:
time: 59 us; the launch traced here: 58.8 us
  Pallas kernels  57.5 us (97%)
  between operations  1.29 us (2%)
    pallas_call x1, Pallas kernels, on_device(): pl.pallas_call(functools.partial(kernel, dims, factor), out_shape=(V((1,...  56.8 us

profile of v4, /device:TPU:1, one launch (start us, length us, event | category | flops | bytes accessed | tf_op | source)
XLA Modules:
  0.0 58.8 jit_solution(187457923381992244)
XLA Ops:
  1.3 56.8 %exchange.1 = (bf16[1,128,512]{2,1,0:T(8,128)(2,1)S(1)}, f32[8,2048]{1,0:T(8,128)S(1)}, f32[1,2048]{1,0:T(1,128)S(1)}) custom-call(bf16[64,2048]{1,0:T(8,128)(2,1)} %hid.1, f32[1,2048]{1,0:T(1,128)} %bitcast.3, bf16[8,2048]{1,0:T(8,128)(2,1)} %wsh.1, bf16[1,128,512]{2,1,0:T(8,128)(2,1)} %cot.1, s32[1]{0:T(128)S(6)} %copy.9.count_ref, s32[1,64]{1,0:T(1,128)} %bitcast.4), custom_call_target="tpu_custom_call" | custom-call | tf_op jit(solution)/shard_map/exchange/pallas_call | solution.py:581
  58.1 0.7 %results.1 = (bf16[1,128,512]{2,1,0:T(8,128)(2,1)}, f32[8,2048]{1,0:T(8,128)}, f32[1,2048]{1,0:T(1,128)}) custom-call(bf16[1,128,512]{2,1,0:T(8,128)(2,1)S(1)} %get-tuple-element.9.k_in, f32[8,2048]{1,0:T(8,128)S(1)} %get-tuple-element.10.gw_in, f32[1,2048]{1,0:T(1,128)S(1)} %get-tuple-element.11.gg_in), custom_call_target="tpu_custom_call" | custom-call | tf_op jit(solution)/shard_map/results/pallas_call | solution.py:604

commit v5 on v4

--- a/solution.py
+++ b/solution.py
@@ -102,6 +102,13 @@
     z_bwd = at_dp(y, lax.rem(z - sign + NZ, NZ), c)
     z_jump = at_dp(y, lax.rem(z + 2 * sign + NZ, NZ), c)
 
+    def y_pair(d):
+        v = y
+        for bit in (1, 2):
+            if d & bit:
+                v = v + bit - 2 * bit * lax.rem(lax.div(y, bit), 2)
+        return v
+
     def zmod(v):
         return lax.rem(v + 2 * NZ, NZ)
 
@@ -243,7 +250,7 @@
                 r_wy[d, dc] = remote(
                     wown.at[:, other_cols if dc else own_cols],
                     wall.at[y, z, c],
-                    at_dp(lax.rem(y + d, NY), z, cc),
+                    at_dp(y_pair(d), z, cc),
                 )
 
     def z_exchange(src, dst):
@@ -273,7 +280,7 @@
     r_h = remote(hown.at[:, other_cols], hbuf.at[c], partner)
 
     def w_send(step, d, fwd, to):
-        yy = lax.rem(y - d + NY, NY)
+        yy = y_pair(d)
         zz = zmod(z - (step - 1) * sign) if fwd else zmod(z + (step - 1) * sign)
         return remote(wall.at[yy, zz], wall.at[yy, zz], to)
 
@@ -385,7 +392,7 @@
     for d in range(NY):
         for step in range(1, LA + 1):
             w_recv(step, d)
-        yy = lax.rem(y - d + NY, NY)
+        yy = y_pair(d)
         block = lax.dot_general(
             norm[...],
             wall[pl.ds(yy, 1)].reshape(kb, half),

time: 59 us -> 58.7 us (level)
  no operation moved by 1% of the time
where the time goes in v5:
time: 58.7 us; the launch traced here: 58.5 us
  Pallas kernels  57.2 us (97%)
  between operations  1.29 us (2%)
    pallas_call x1, Pallas kernels, on_device(): pl.pallas_call(functools.partial(kernel, dims, factor), out_shape=(V((1,...  56.5 us

profile of v5, /device:TPU:1, one launch (start us, length us, event | category | flops | bytes accessed | tf_op | source)
XLA Modules:
  0.0 58.5 jit_solution(2177458912693618752)
XLA Ops:
  1.3 56.5 %exchange.1 = (bf16[1,128,512]{2,1,0:T(8,128)(2,1)S(1)}, f32[8,2048]{1,0:T(8,128)S(1)}, f32[1,2048]{1,0:T(1,128)S(1)}) custom-call(bf16[64,2048]{1,0:T(8,128)(2,1)} %hid.1, f32[1,2048]{1,0:T(1,128)} %bitcast.3, bf16[8,2048]{1,0:T(8,128)(2,1)} %wsh.1, bf16[1,128,512]{2,1,0:T(8,128)(2,1)} %cot.1, s32[1]{0:T(128)S(6)} %copy.9.count_ref, s32[1,64]{1,0:T(1,128)} %bitcast.4), custom_call_target="tpu_custom_call" | custom-call | tf_op jit(solution)/shard_map/exchange/pallas_call | solution.py:588
  57.8 0.7 %results.1 = (bf16[1,128,512]{2,1,0:T(8,128)(2,1)}, f32[8,2048]{1,0:T(8,128)}, f32[1,2048]{1,0:T(1,128)}) custom-call(bf16[1,128,512]{2,1,0:T(8,128)(2,1)S(1)} %get-tuple-element.9.k_in, f32[8,2048]{1,0:T(8,128)S(1)} %get-tuple-element.10.gw_in, f32[1,2048]{1,0:T(1,128)S(1)} %get-tuple-element.11.gg_in), custom_call_target="tpu_custom_call" | custom-call | tf_op jit(solution)/shard_map/results/pallas_call | solution.py:611
